TPU v7x, 256 devices: a whole 4x4x8 slice. The times are simulated.
256 devices in a mesh: seq: 128 (over y, z, x), batch: 2 (over core).
Axes of the slice: x: 4, y: 4, z: 8, core: 2. Of those that a mesh axis runs over, the one named last changes fastest.
Arguments:
- points: bfloat16 [2, 131072, 256], P('batch', 'seq'), may hold values from -6 to 6
- gain: float32 [256], replicated, may hold values from 0.5 to 1.5
- w_qkv: bfloat16 [256, 768], replicated
- w_out: bfloat16 [256, 256], replicated, may hold values from -0.375 to 0.375
- route: int32 [2, 1024], P('batch', 'seq'), may hold values from 0 to 1023, as said below
- order: int32 [2, 128, 1024], P('batch', 'seq'), may hold values from 0 to 1023, each once within a row
- pattern: int32 [2, 256, 4, 4], P('batch', 'seq'), may hold values 0 or 1
- grad_out: bfloat16 [2, 131072, 256], P('batch', 'seq'), may hold values from -6 to 6
Outputs:
- result: bfloat16 [2, 131072, 256], P('batch', 'seq')
- grad_points: bfloat16 [2, 131072, 256], P('batch', 'seq')
- grad_gain: float32 [256], replicated
- grad_w_qkv: float32 [256, 768], replicated
- grad_w_out: float32 [256, 256], replicated
Inputs may be any that keep to these rules, and one draw needn't show every extreme that they name: For each sample, route is a permutation of the 1024 slot numbers. Slot s goes to a device (route // 8) within 2 of its own device s // 8; one device sends at most 2 slots to any one other device and receives as many back from it; in every sample some pair of devices exchanges exactly 2.
All inputs are finite; a program needn't handle non-finite values. No bound on the sum of `pattern` on one device may be relied on, other than what follows from the above.
Results may differ from a plain program's by a relative error of at most 0.0085.
The roundings to bfloat16 on the way count: a program that leaves them out, or rounds other values in their place, can miss the bound.
Values may be sent and summed in bfloat16 or wider, within the bound.
No kernel may reach another device: no remote copies, remote signals or barrier semaphores. Data moves between devices by JAX's collectives and lax.ppermute only.
A program may use at most 128 MiB of HBM per device.

v0:
```python
import jax
import jax.numpy as jnp
from jax import lax
from jax.sharding import PartitionSpec as P

HEADS = 8
WINDOW = 512
SLOT = 128
HOP = 2
MOST = 2
EPSILON = 1e-05


def from_behind(array, axis, by):
    peers = lax.axis_size(axis)
    pairs = [(i, i + by) for i in range(peers) if 0 <= i + by < peers]
    return lax.ppermute(array, axis, pairs)


def multiply(form, left, right):
    return jnp.einsum(form, left, right, preferred_element_type=jnp.float32)


def norm_stats(window_rows):
    as_float = window_rows.astype(jnp.float32)
    centred = as_float - jnp.mean(as_float, axis=-1, keepdims=True)
    inverse_std = lax.rsqrt(jnp.mean(centred * centred, axis=-1, keepdims=True) + EPSILON)
    return (as_float, centred * inverse_std, inverse_std)


def block_probs(qkv, allowed, start, amount, heads, slot):
    total_rows = qkv.shape[0]
    width = qkv.shape[1] // 3
    head_dim = width // heads
    queries = qkv[start : start + amount, :width].reshape(amount, heads, head_dim)
    keys_all = qkv[:, width : 2 * width].reshape(total_rows, heads, head_dim)
    scores = multiply("qhd,khd->hqk", queries, keys_all) * head_dim ** (-0.5)
    block_rows = jnp.repeat(allowed, slot, axis=0)
    visible = jnp.repeat(block_rows, slot, axis=1)
    scores = jnp.where(visible[None], scores, -jnp.inf)
    highest = jnp.max(scores, axis=-1, keepdims=True)
    powers = jnp.exp(scores - highest)
    return powers / jnp.sum(powers, axis=-1, keepdims=True)


def window_forward(window_rows, gain, w_qkv, w_out, allowed, heads, slot):
    as_float, normalized, inverse_std = norm_stats(window_rows)
    normed = (normalized * gain).astype(jnp.bfloat16)
    qkv = jnp.dot(normed, w_qkv, preferred_element_type=jnp.float32).astype(jnp.bfloat16)
    total_rows, width = window_rows.shape
    head_dim = width // heads
    values_all = qkv[:, 2 * width :].reshape(total_rows, heads, head_dim)
    query_step = min(512, total_rows)
    probs = block_probs(qkv, allowed, 0, query_step, heads, slot)
    kept_probs = [probs]
    rounded = probs.astype(jnp.bfloat16)
    blended = multiply("hqk,khd->qhd", rounded, values_all)
    pieces = blended.reshape(query_step, width).astype(jnp.bfloat16)
    output = (as_float + jnp.dot(pieces, w_out, preferred_element_type=jnp.float32)).astype(
        jnp.bfloat16
    )
    return (output, (normed, qkv, pieces, normalized, inverse_std, kept_probs))


def window_backward(grad_rows, gain, w_qkv, w_out, saved, heads):
    normed, qkv, mixed, normalized, inverse_std, kept_probs = saved
    total_rows, width = grad_rows.shape
    head_dim = width // heads
    d_mixed = jnp.dot(grad_rows, w_out.T, preferred_element_type=jnp.float32).astype(jnp.bfloat16)
    g_out = jnp.dot(mixed.T, grad_rows, preferred_element_type=jnp.float32)
    queries = qkv[:, :width].reshape(total_rows, heads, head_dim)
    keys_all = qkv[:, width : 2 * width].reshape(total_rows, heads, head_dim)
    values_all = qkv[:, 2 * width :].reshape(total_rows, heads, head_dim)
    d_keys = jnp.zeros((total_rows, heads, head_dim), jnp.float32)
    d_values = jnp.zeros((total_rows, heads, head_dim), jnp.float32)
    query_step = min(512, total_rows)
    d_query_parts = []
    for number, start in enumerate(range(0, total_rows, query_step)):
        probs = kept_probs[number]
        rounded = probs.astype(jnp.bfloat16)
        d_block = d_mixed.reshape(query_step, heads, head_dim)
        d_values = multiply("hqk,qhd->khd", rounded, d_block)
        d_probs = multiply("qhd,khd->hqk", d_block, values_all)
        d_scores = (
            probs
            * (d_probs - jnp.sum(d_probs * probs, axis=-1, keepdims=True))
            * head_dim ** (-0.5)
        )
        d_scores = d_scores.astype(jnp.bfloat16)
        d_query_parts.append(
            multiply("hqk,khd->qhd", d_scores, keys_all).reshape(query_step, width)
        )
        d_keys = multiply("hqk,qhd->khd", d_scores, queries)
    d_qkv = jnp.concatenate(
        [d_query_parts[0], d_keys.reshape(total_rows, width), d_values.reshape(total_rows, width)],
        axis=1,
    ).astype(jnp.bfloat16)
    g_qkv = jnp.dot(normed.T, d_qkv, preferred_element_type=jnp.float32)
    d_normed = jnp.dot(d_qkv, w_qkv.T, preferred_element_type=jnp.float32)
    g_gain = jnp.sum(d_normed * normalized, axis=0)
    d_hat = d_normed * gain
    branch = inverse_std * (
        d_hat
        - jnp.mean(d_hat, axis=-1, keepdims=True)
        - normalized * jnp.mean(d_hat * normalized, axis=-1, keepdims=True)
    )
    d_rows = (grad_rows.astype(jnp.float32) + branch).astype(jnp.bfloat16)
    return (d_rows, g_gain, g_qkv, g_out)


def pack_slots(slots, offsets, targets, positions, distance):
    matching = offsets == distance
    ranking = jnp.cumsum(matching.astype(jnp.int32)) - 1
    chosen = matching[None, :] & (ranking[None, :] == jnp.arange(MOST, dtype=jnp.int32)[:, None])
    packed = multiply("mc,csd->msd", chosen.astype(jnp.bfloat16), slots).astype(jnp.bfloat16)
    landing = jnp.sum(jnp.where(chosen, targets[None, :] + 1, 0), axis=1)
    anchor = jnp.sum(jnp.where(chosen, positions[None, :], 0), axis=1)
    labels = jnp.stack([landing, anchor]).astype(jnp.bfloat16)
    return (packed, labels)


def relocate(slots, offsets, targets):
    amount = slots.shape[0]
    positions = jnp.arange(amount, dtype=jnp.int32)
    blocks = [slots]
    landings = [jnp.where(offsets == 0, targets, -1)]
    sources = [jnp.zeros((amount,), jnp.int32)]
    anchors = [positions]

    def receive(arrived_rows, arrived_labels, source_offset):
        blocks.append(arrived_rows)
        landings.append(arrived_labels[0].astype(jnp.int32) - 1)
        sources.append(jnp.full((MOST,), source_offset, jnp.int32))
        anchors.append(arrived_labels[1].astype(jnp.int32))

    for distance in [value for value in range(-HOP, HOP + 1) if value != 0]:
        packed, labels = pack_slots(slots, offsets, targets, positions, distance)
        arrived_rows, arrived_labels = from_behind((packed, labels), "seq", distance)
        receive(arrived_rows, arrived_labels, -distance)
    every_row = jnp.concatenate(blocks, axis=0)
    every_landing = jnp.concatenate(landings)
    placement = every_landing[None, :] == positions[:, None]
    arrived = multiply("pc,csd->psd", placement.astype(jnp.bfloat16), every_row).astype(
        jnp.bfloat16
    )
    from_offset = jnp.sum(jnp.where(placement, jnp.concatenate(sources)[None, :], 0), axis=1)
    from_spot = jnp.sum(jnp.where(placement, jnp.concatenate(anchors)[None, :], 0), axis=1)
    return (arrived, from_offset, from_spot)


def body(points, gain, w_qkv, w_out, route, order, pattern, grad_out):
    local_rows = points[0]
    total_rows, width = local_rows.shape
    amount = total_rows // SLOT
    device_here = lax.axis_index("seq")
    targets = route[0]
    offsets = targets // amount - device_here
    spots = targets % amount
    together = jnp.concatenate([local_rows, grad_out[0]], axis=1).reshape(amount, SLOT, 2 * width)
    arrived, from_offset, from_spot = relocate(together, offsets, spots)
    picking = order[0, 0]
    arrived_rows = arrived.reshape(total_rows, 2 * width)[picking]
    hilbert = arrived_rows[:, :width]
    upstream = arrived_rows[:, width:]
    blocks_total = pattern.shape[2]
    allowed = (pattern[0] > 0) | jnp.eye(blocks_total, dtype=bool)[None]
    out_parts = []
    grad_parts = []
    sum_gain = jnp.zeros((width,), jnp.float32)
    sum_qkv = jnp.zeros((width, 3 * width), jnp.float32)
    sum_out = jnp.zeros((width, width), jnp.float32)
    for number in range(total_rows // WINDOW):
        first_row = number * WINDOW
        output, saved = window_forward(
            hilbert[first_row : first_row + WINDOW],
            gain,
            w_qkv,
            w_out,
            allowed[number],
            HEADS,
            SLOT,
        )
        d_rows, g_gain, g_qkv, g_out = window_backward(
            upstream[first_row : first_row + WINDOW], gain, w_qkv, w_out, saved, HEADS
        )
        out_parts.append(output)
        grad_parts.append(d_rows)
        sum_gain = sum_gain + g_gain
        sum_qkv = sum_qkv + g_qkv
        sum_out = sum_out + g_out
    out_hilbert = jnp.concatenate(out_parts, axis=0)
    grad_hilbert = jnp.concatenate(grad_parts, axis=0)
    inverse_order = (
        jnp.zeros((total_rows,), jnp.int32).at[picking].set(jnp.arange(total_rows, dtype=jnp.int32))
    )
    leaving = jnp.concatenate([out_hilbert, grad_hilbert], axis=1)[inverse_order].reshape(
        amount, SLOT, 2 * width
    )
    returned, ignore_a, ignore_b = relocate(leaving, from_offset, from_spot)
    returned = returned.reshape(total_rows, 2 * width)
    sum_gain, sum_qkv, sum_out = lax.psum((sum_gain, sum_qkv, sum_out), ("seq", "batch"))
    factor = (lax.axis_size("batch") * lax.axis_size("seq") * total_rows) ** (-0.5)
    result = returned[:, :width].reshape(1, total_rows, width)
    grad_points = returned[:, width:].reshape(1, total_rows, width)
    return (result, grad_points, sum_gain * factor, sum_qkv * factor, sum_out * factor)


def solution(mesh):
    return jax.shard_map(
        body,
        mesh=mesh,
        in_specs=(
            P("batch", "seq", None),
            P(),
            P(),
            P(),
            P("batch", "seq"),
            P("batch", "seq", None),
            P("batch", "seq", None, None),
            P("batch", "seq", None),
        ),
        out_specs=(P("batch", "seq", None), P("batch", "seq", None), P(), P(), P()),
        check_vma=False,
    )
```

profile of v0, /device:TPU:2, one launch (start us, length us, event | category | flops | bytes accessed | tf_op | source)
XLA Modules:
  0.0 501.4 jit_solution(3498689452637965168)
XLA Ops:
  11.0 6.2 %collective-permute-start.2 = (bf16[2,2]{1,0:T(2,128)(2,1)S(1)}, bf16[2,2]{1,0:T(2,128)(2,1)S(1)}, u32[]{:S(2)}, u32[]{:S(2)}) collective-permute-start(bf16[2,2]{1,0:T(2,128)(2,1)S(1)} %pad_maximum_fusion.8), channel_id=1, source_target_pairs={{0,2},{2,4},{4,6},{6,8},{8,10},{10,12},{12,14},{14,16},{16,18},{18... | collective-permute-start | bytes 32 | tf_op jit(solution)/shard_map/ppermute | solution.py:17
  19.2 4.7 collective-permute-start.3
  33.1 4.3 scatter_custom_fusion
  38.3 4.2 collective-permute-start.10
  42.5 4.6 collective-permute-start.11
  51.2 6.1 %collective-permute-start.7 = (bf16[2,2]{1,0:T(2,128)(2,1)S(1)}, bf16[2,2]{1,0:T(2,128)(2,1)S(1)}, u32[]{:S(2)}, u32[]{:S(2)}) collective-permute-start(bf16[2,2]{1,0:T(2,128)(2,1)S(1)} %pad_maximum_fusion.13), channel_id=1, source_target_pairs={{0,4},{2,6},{4,8},{6,10},{8,12},{10,14},{12,16},{14,18},{16,20},{1... | collective-permute-start | bytes 32 | tf_op jit(solution)/shard_map/ppermute | solution.py:17
  59.8 5.9 %collective-permute-done.4 = bf16[2,2]{1,0:T(2,128)(2,1)S(1)} collective-permute-done((bf16[2,2]{1,0:T(2,128)(2,1)S(1)}, bf16[2,2]{1,0:T(2,128)(2,1)S(1)}, u32[]{:S(2)}, u32[]{:S(2)}) %collective-permute-start.4) | collective-permute-done | bytes 40 | tf_op jit(solution)/shard_map/ppermute | solution.py:17
  65.7 5.7 %collective-permute-start.6 = (bf16[2,2]{1,0:T(2,128)(2,1)S(1)}, bf16[2,2]{1,0:T(2,128)(2,1)S(1)}, u32[]{:S(2)}, u32[]{:S(2)}) collective-permute-start(bf16[2,2]{1,0:T(2,128)(2,1)S(1)} %pad_maximum_fusion.12), channel_id=1, source_target_pairs={{0,2},{2,4},{4,6},{6,8},{8,10},{10,12},{12,14},{14,16},{16,18},{18... | collective-permute-start | bytes 32 | tf_op jit(solution)/shard_map/ppermute | solution.py:17
  80.5 4.5 concatenate.46
  86.5 4.0 gather_fusion
  92.7 5.4 %fusion.155 = (f32[8,512]{1,0:T(8,128)S(1)}, f32[8,512,512]{1,2,0:T(8,128)}) fusion(pred[512,512]{0,1:T(8,128)(4,1)S(1)} %bitcast.277, bf16[512,8,32]{0,2,1:T(8,128)(2,1)S(1)} %bitcast.271, bf16[512,8,32]{0,2,1:T(8,128)(2,1)S(1)} %bitcast.269), kind=kOutput, calls=%fused_computation.286 | convolution fusion | flops 142606848 | bytes 9191424 | tf_op jit(solution)/shard_map/sub | solution.py:42
  98.1 4.4 fusion.50
  105.7 4.5 fusion.157
  110.2 14.7 %fusion.44 = bf16[8,32,512]{2,1,0:T(8,128)(2,1)} fusion(bf16[512,8,32]{0,2,1:T(8,128)(2,1)S(1)} %bitcast.270, f32[8,512,512]{1,2,0:T(8,128)} %fusion.157, f32[8,512,512]{1,2,0:T(8,128)} %get-tuple-element.79, f32[8,512]{1,0:T(8,128)S(1)} %get-tuple-element.78), kind=kOutput, calls=%fused_computation.48 | convolution fusion | flops 149033472 | bytes 17317888 | tf_op jit(solution)/shard_map/hqk,khd->qhd/dot_general | solution.py:21
  124.9 12.8 %fusion.47 = bf16[8,32,512]{2,1,0:T(8,128)(2,1)} fusion(bf16[512,8,32]{0,2,1:T(8,128)(2,1)S(1)} %bitcast.272, f32[8,512,512]{1,2,0:T(8,128)} %fusion.157, f32[8,512,512]{1,2,0:T(8,128)} %get-tuple-element.79, f32[8,512]{1,0:T(8,128)S(1)} %get-tuple-element.78), kind=kOutput, calls=%fused_computation.49 | convolution fusion | flops 149033472 | bytes 17317888 | tf_op jit(solution)/shard_map/hqk,qhd->khd/dot_general | solution.py:21
  138.8 5.4 %fusion.156 = (f32[8,512]{1,0:T(8,128)S(1)}, f32[8,512,512]{1,2,0:T(8,128)}) fusion(pred[512,512]{0,1:T(8,128)(4,1)S(1)} %bitcast.278, bf16[512,8,32]{0,2,1:T(8,128)(2,1)S(1)} %bitcast.275, bf16[512,8,32]{0,2,1:T(8,128)(2,1)S(1)} %bitcast.273), kind=kOutput, calls=%fused_computation.287 | convolution fusion | flops 142606848 | bytes 9191424 | tf_op jit(solution)/shard_map/sub | solution.py:42
  144.1 5.6 %fusion.59 = bf16[8,32,512]{2,1,0:T(8,128)(2,1)} fusion(bf16[512,8,32]{0,2,1:T(8,128)(2,1)S(1)} %bitcast.257, f32[8,512,512]{1,2,0:T(8,128)} %get-tuple-element.81, f32[8,512]{1,0:T(8,128)S(1)} %get-tuple-element.80), kind=kOutput, calls=%fused_computation.53 | convolution fusion | flops 138543104 | bytes 8929280 | tf_op jit(solution)/shard_map/hqk,qhd->khd/dot_general | solution.py:21
  150.8 4.5 fusion.158
  155.3 14.7 %fusion.38 = bf16[8,32,512]{2,1,0:T(8,128)(2,1)} fusion(bf16[512,8,32]{0,2,1:T(8,128)(2,1)S(1)} %bitcast.274, f32[8,512,512]{1,2,0:T(8,128)} %fusion.158, f32[8,512,512]{1,2,0:T(8,128)} %get-tuple-element.81, f32[8,512]{1,0:T(8,128)S(1)} %get-tuple-element.80), kind=kOutput, calls=%fused_computation.46 | convolution fusion | flops 149033472 | bytes 17317888 | tf_op jit(solution)/shard_map/hqk,khd->qhd/dot_general | solution.py:21
  170.0 12.8 %fusion.41 = bf16[8,32,512]{2,1,0:T(8,128)(2,1)} fusion(bf16[512,8,32]{0,2,1:T(8,128)(2,1)S(1)} %bitcast.276, f32[8,512,512]{1,2,0:T(8,128)} %fusion.158, f32[8,512,512]{1,2,0:T(8,128)} %get-tuple-element.81, f32[8,512]{1,0:T(8,128)S(1)} %get-tuple-element.80), kind=kOutput, calls=%fused_computation.47 | convolution fusion | flops 149033472 | bytes 17317888 | tf_op jit(solution)/shard_map/hqk,qhd->khd/dot_general | solution.py:21
  200.8 6.7 %collective-permute-start.15 = (bf16[2,128,512]{2,0,1:T(2,128)(2,1)}, bf16[2,128,512]{2,0,1:T(2,128)(2,1)S(1)}, u32[]{:S(2)}, u32[]{:S(2)}) collective-permute-start(bf16[2,128,512]{2,0,1:T(2,128)(2,1)} %convolution_convert_fusion.4), channel_id=1, source_target_pairs={{0,4},{2,6},{4,8},{6,10},{8,12},{10,14},{12,16},{14,18},{16,20},{1... | collective-permute-start | bytes 786440 | tf_op jit(solution)/shard_map/ppermute | solution.py:17
  217.9 90.1 %psum.21 = f32[256]{0:T(256)S(1)} all-reduce(f32[256]{0:T(256)S(1)} %add.179), channel_id=1, replica_groups=mesh['seq'=128,'batch'=2] {'seq','batch'}, use_global_device_ids=true, to_apply=%region_43.44 | all-reduce | flops 256 | bytes 2048 | tf_op jit(solution)/shard_map/psum | solution.py:201
  309.4 4.5 concatenate.52
  315.7 174.9 %all-reduce.3.cloned.1.call-done = (f32[256,768]{1,0:T(8,128)}, f32[256,256]{1,0:T(8,128)}) async-done(((f32[256,768]{1,0:T(8,128)}, f32[256,256]{1,0:T(8,128)}), (f32[256,768]{1,0:T(8,128)}, f32[256,256]{1,0:T(8,128)})) %all-reduce.3.cloned.1.call-update) | async-done | bytes 1048592 | tf_op jit(solution)/shard_map/psum | solution.py:201
  (199 shorter events, 75.2 us)
Async XLA Ops:
  7.2 84.5 %copy-start = (bf16[256,768]{1,0:T(8,128)(2,1)S(1)}, bf16[256,768]{1,0:T(8,128)(2,1)}, u32[]{:S(2)}) copy-start(bf16[256,768]{1,0:T(8,128)(2,1)} %param.10) | copy-start | bytes 1179652
  7.2 483.4 %all-reduce.3.cloned.1.call-start = ((), (), s32[]{:S(2)}) async-start(), calls=%async_computation | async-start | bytes 2097152 | tf_op jit(solution)/shard_map/psum | solution.py:201
  9.6 28.7 %collective-permute-start = (bf16[2,2]{1,0:T(2,128)(2,1)S(1)}, bf16[2,2]{1,0:T(2,128)(2,1)S(1)}, u32[]{:S(2)}, u32[]{:S(2)}) collective-permute-start(bf16[2,2]{1,0:T(2,128)(2,1)S(1)} %pad_maximum_fusion.6), channel_id=1, source_target_pairs={{4,0},{6,2},{8,4},{10,6},{12,8},{14,10},{16,12},{18,14},{20,16},{2... | collective-permute-start | bytes 32 | tf_op jit(solution)/shard_map/ppermute | solution.py:17
  11.0 31.6 %collective-permute-start.2 = (bf16[2,2]{1,0:T(2,128)(2,1)S(1)}, bf16[2,2]{1,0:T(2,128)(2,1)S(1)}, u32[]{:S(2)}, u32[]{:S(2)}) collective-permute-start(bf16[2,2]{1,0:T(2,128)(2,1)S(1)} %pad_maximum_fusion.8), channel_id=1, source_target_pairs={{0,2},{2,4},{4,6},{6,8},{8,10},{10,12},{12,14},{14,16},{16,18},{18... | collective-permute-start | bytes 32 | tf_op jit(solution)/shard_map/ppermute | solution.py:17
  17.2 29.9 %collective-permute-start.1 = (bf16[2,2]{1,0:T(2,128)(2,1)S(1)}, bf16[2,2]{1,0:T(2,128)(2,1)S(1)}, u32[]{:S(2)}, u32[]{:S(2)}) collective-permute-start(bf16[2,2]{1,0:T(2,128)(2,1)S(1)} %pad_maximum_fusion.7), channel_id=1, source_target_pairs={{2,0},{4,2},{6,4},{8,6},{10,8},{12,10},{14,12},{16,14},{18,16},{20... | collective-permute-start | bytes 32 | tf_op jit(solution)/shard_map/ppermute | solution.py:17
  19.2 29.3 %collective-permute-start.3 = (bf16[2,2]{1,0:T(2,128)(2,1)S(1)}, bf16[2,2]{1,0:T(2,128)(2,1)S(1)}, u32[]{:S(2)}, u32[]{:S(2)}) collective-permute-start(bf16[2,2]{1,0:T(2,128)(2,1)S(1)} %pad_maximum_fusion.9), channel_id=1, source_target_pairs={{0,4},{2,6},{4,8},{6,10},{8,12},{10,14},{12,16},{14,18},{16,20},{1... | collective-permute-start | bytes 32 | tf_op jit(solution)/shard_map/ppermute | solution.py:17
  27.0 52.0 %collective-permute-start.9 = (bf16[2,128,512]{2,0,1:T(2,128)(2,1)S(1)}, bf16[2,128,512]{2,0,1:T(2,128)(2,1)S(1)}, u32[]{:S(2)}, u32[]{:S(2)}) collective-permute-start(bf16[2,128,512]{2,0,1:T(2,128)(2,1)S(1)} %convolution_convert_fusion.12), channel_id=1, source_target_pairs={{2,0},{4,2},{6,4},{8,6},{10,8},{12,10},{14,12},{16,14},{18,16},{20... | collective-permute-start | bytes 786440 | tf_op jit(solution)/shard_map/ppermute | solution.py:17
  38.3 40.7 %collective-permute-start.10 = (bf16[2,128,512]{2,0,1:T(2,128)(2,1)S(1)}, bf16[2,128,512]{2,0,1:T(2,128)(2,1)S(1)}, u32[]{:S(2)}, u32[]{:S(2)}) collective-permute-start(bf16[2,128,512]{2,0,1:T(2,128)(2,1)S(1)} %convolution_convert_fusion.11), channel_id=1, source_target_pairs={{0,2},{2,4},{4,6},{6,8},{8,10},{10,12},{12,14},{14,16},{16,18},{18... | collective-permute-start | bytes 786440 | tf_op jit(solution)/shard_map/ppermute | solution.py:17
  42.5 36.5 %collective-permute-start.11 = (bf16[2,128,512]{2,0,1:T(2,128)(2,1)S(1)}, bf16[2,128,512]{2,0,1:T(2,128)(2,1)S(1)}, u32[]{:S(2)}, u32[]{:S(2)}) collective-permute-start(bf16[2,128,512]{2,0,1:T(2,128)(2,1)S(1)} %convolution_convert_fusion.10), channel_id=1, source_target_pairs={{0,4},{2,6},{4,8},{6,10},{8,12},{10,14},{12,16},{14,18},{16,20},{1... | collective-permute-start | bytes 786440 | tf_op jit(solution)/shard_map/ppermute | solution.py:17
  47.1 33.4 %collective-permute-start.8 = (bf16[2,128,512]{2,0,1:T(2,128)(2,1)S(1)}, bf16[2,128,512]{2,0,1:T(2,128)(2,1)}, u32[]{:S(2)}, u32[]{:S(2)}) collective-permute-start(bf16[2,128,512]{2,0,1:T(2,128)(2,1)S(1)} %convolution_convert_fusion.13), channel_id=1, source_target_pairs={{4,0},{6,2},{8,4},{10,6},{12,8},{14,10},{16,12},{18,14},{20,16},{2... | collective-permute-start | bytes 786440 | tf_op jit(solution)/shard_map/ppermute | solution.py:17
  49.5 29.6 %copy-start.9 = (pred[8]{0:T(512)(128)(4,1)}, pred[8]{0:T(512)(128)(4,1)S(1)}, u32[]{:S(2)}) copy-start(pred[8]{0:T(512)(128)(4,1)S(1)} %get-tuple-element.70) | copy-start | bytes 28
  49.9 29.2 %copy-start.12 = (s32[8]{0:T(128)}, s32[8]{0:T(128)S(1)}, u32[]{:S(2)}) copy-start(s32[8]{0:T(128)S(1)} %add_bitcast_fusion.7) | copy-start | bytes 100
  51.2 7.3 %collective-permute-start.7 = (bf16[2,2]{1,0:T(2,128)(2,1)S(1)}, bf16[2,2]{1,0:T(2,128)(2,1)S(1)}, u32[]{:S(2)}, u32[]{:S(2)}) collective-permute-start(bf16[2,2]{1,0:T(2,128)(2,1)S(1)} %pad_maximum_fusion.13), channel_id=1, source_target_pairs={{0,4},{2,6},{4,8},{6,10},{8,12},{10,14},{12,16},{14,18},{16,20},{1... | collective-permute-start | bytes 32 | tf_op jit(solution)/shard_map/ppermute | solution.py:17
  58.5 7.2 %collective-permute-start.4 = (bf16[2,2]{1,0:T(2,128)(2,1)S(1)}, bf16[2,2]{1,0:T(2,128)(2,1)S(1)}, u32[]{:S(2)}, u32[]{:S(2)}) collective-permute-start(bf16[2,2]{1,0:T(2,128)(2,1)S(1)} %pad_maximum_fusion.10), channel_id=1, source_target_pairs={{4,0},{6,2},{8,4},{10,6},{12,8},{14,10},{16,12},{18,14},{20,16},{2... | collective-permute-start | bytes 32 | tf_op jit(solution)/shard_map/ppermute | solution.py:17
  65.7 7.0 %collective-permute-start.6 = (bf16[2,2]{1,0:T(2,128)(2,1)S(1)}, bf16[2,2]{1,0:T(2,128)(2,1)S(1)}, u32[]{:S(2)}, u32[]{:S(2)}) collective-permute-start(bf16[2,2]{1,0:T(2,128)(2,1)S(1)} %pad_maximum_fusion.12), channel_id=1, source_target_pairs={{0,2},{2,4},{4,6},{6,8},{8,10},{10,12},{12,14},{14,16},{16,18},{18... | collective-permute-start | bytes 32 | tf_op jit(solution)/shard_map/ppermute | solution.py:17
  72.7 5.7 %collective-permute-start.5 = (bf16[2,2]{1,0:T(2,128)(2,1)S(1)}, bf16[2,2]{1,0:T(2,128)(2,1)S(1)}, u32[]{:S(2)}, u32[]{:S(2)}) collective-permute-start(bf16[2,2]{1,0:T(2,128)(2,1)S(1)} %pad_maximum_fusion.11), channel_id=1, source_target_pairs={{2,0},{4,2},{6,4},{8,6},{10,8},{12,10},{14,12},{16,14},{18,16},{20... | collective-permute-start | bytes 32 | tf_op jit(solution)/shard_map/ppermute | solution.py:17
  150.7 32.1 %copy-start.7 = (bf16[8,32,512]{2,1,0:T(8,128)(2,1)}, bf16[8,32,512]{2,1,0:T(8,128)(2,1)S(1)}, u32[]{:S(2)}) copy-start(bf16[8,32,512]{2,1,0:T(8,128)(2,1)S(1)} %fusion.56) | copy-start | bytes 786436
  169.9 13.1 %copy-start.17 = (bf16[8,32,512]{2,1,0:T(8,128)(2,1)S(1)}, bf16[8,32,512]{2,1,0:T(8,128)(2,1)}, u32[]{:S(2)}) copy-start(bf16[8,32,512]{2,1,0:T(8,128)(2,1)} %fusion.44) | copy-start | bytes 786436
  191.1 8.3 %copy-start.14 = (pred[2,8]{1,0:T(4,128)(4,1)S(1)}, pred[2,8]{1,0:T(4,128)(4,1)}, u32[]{:S(2)}) copy-start(pred[2,8]{1,0:T(4,128)(4,1)} %get-tuple-element.41) | copy-start | bytes 52
  195.1 118.8 %copy-start.15 = (s32[16]{0:T(128)S(1)}, s32[16]{0:T(128)}, u32[]{:S(2)}) copy-start(s32[16]{0:T(128)} %concatenate.42) | copy-start | bytes 196
  200.8 107.8 %collective-permute-start.15 = (bf16[2,128,512]{2,0,1:T(2,128)(2,1)}, bf16[2,128,512]{2,0,1:T(2,128)(2,1)S(1)}, u32[]{:S(2)}, u32[]{:S(2)}) collective-permute-start(bf16[2,128,512]{2,0,1:T(2,128)(2,1)} %convolution_convert_fusion.4), channel_id=1, source_target_pairs={{0,4},{2,6},{4,8},{6,10},{8,12},{10,14},{12,16},{14,18},{16,20},{1... | collective-permute-start | bytes 786440 | tf_op jit(solution)/shard_map/ppermute | solution.py:17
  207.5 101.1 %collective-permute-start.14 = (bf16[2,128,512]{2,0,1:T(2,128)(2,1)S(1)}, bf16[2,128,512]{2,0,1:T(2,128)(2,1)S(1)}, u32[]{:S(2)}, u32[]{:S(2)}) collective-permute-start(bf16[2,128,512]{2,0,1:T(2,128)(2,1)S(1)} %convolution_convert_fusion.5), channel_id=1, source_target_pairs={{0,2},{2,4},{4,6},{6,8},{8,10},{10,12},{12,14},{14,16},{16,18},{18... | collective-permute-start | bytes 786440 | tf_op jit(solution)/shard_map/ppermute | solution.py:17
  210.1 98.5 %collective-permute-start.13 = (bf16[2,128,512]{2,0,1:T(2,128)(2,1)S(1)}, bf16[2,128,512]{2,0,1:T(2,128)(2,1)}, u32[]{:S(2)}, u32[]{:S(2)}) collective-permute-start(bf16[2,128,512]{2,0,1:T(2,128)(2,1)S(1)} %convolution_convert_fusion.6), channel_id=1, source_target_pairs={{2,0},{4,2},{6,4},{8,6},{10,8},{12,10},{14,12},{16,14},{18,16},{20... | collective-permute-start | bytes 786440 | tf_op jit(solution)/shard_map/ppermute | solution.py:17
  213.4 96.0 %collective-permute-start.12 = (bf16[2,128,512]{2,0,1:T(2,128)(2,1)}, bf16[2,128,512]{2,0,1:T(2,128)(2,1)}, u32[]{:S(2)}, u32[]{:S(2)}) collective-permute-start(bf16[2,128,512]{2,0,1:T(2,128)(2,1)} %convolution_convert_fusion.7), channel_id=1, source_target_pairs={{4,0},{6,2},{8,4},{10,6},{12,8},{14,10},{16,12},{18,14},{20,16},{2... | collective-permute-start | bytes 786440 | tf_op jit(solution)/shard_map/ppermute | solution.py:17
  (14 other events, 50.4 us)
Sparse Core Ops, SparseCore 0:
  218.0 272.5 all-reduce.2
where the time goes:
time: 507 us; the launch traced here: 501 us
  waiting for transfers between devices  187 us (37%)
  matrix products  108 us (21%)
  blocking collectives  90.1 us (18%)
  starting transfers between devices  56.6 us (11%)
  local copies, waits for them, and re-layouts  30.9 us (6%)
  between operations  15.2 us (3%)
  other arithmetic  13.5 us (3%)
    psum x1, waiting for transfers between devices, body(): lax.psum((sum_gain, sum_qkv, sum_out), ('seq', 'batch'))  175 us
    psum x1, blocking collectives, body(): lax.psum((sum_gain, sum_qkv, sum_out), ('seq', 'batch'))  90.1 us
    dot_general x20, matrix products, multiply(): return jnp.einsum(form, left, right, preferred_element_type=jnp.float32)  85 us
    ppermute x16, starting transfers between devices, from_behind(): return lax.ppermute(array, axis, pairs)  56.6 us
    ppermute x16, waiting for transfers between devices, from_behind(): return lax.ppermute(array, axis, pairs)  11.8 us
    sub x2, matrix products, block_probs(): powers = jnp.exp(scores - highest)  10.7 us
  transfers between devices with their start and end apart: 17, of which 5 were waited for; matrix products, arithmetic and copies ran while one was open for 5% of the time, Pallas kernels for 0%

commit v1 on v0

--- a/solution.py
+++ b/solution.py
@@ -198,7 +198,7 @@
     )
     returned, ignore_a, ignore_b = relocate(leaving, from_offset, from_spot)
     returned = returned.reshape(total_rows, 2 * width)
-    sum_gain, sum_qkv, sum_out = lax.psum((sum_gain, sum_qkv, sum_out), ("seq", "batch"))
+    sum_gain, sum_qkv, sum_out = lax.psum(lax.psum((sum_gain, sum_qkv, sum_out), "seq"), "batch")
     factor = (lax.axis_size("batch") * lax.axis_size("seq") * total_rows) ** (-0.5)
     result = returned[:, :width].reshape(1, total_rows, width)
     grad_points = returned[:, width:].reshape(1, total_rows, width)

time: 507 us -> 813 us (1.60)
  blocking collectives: 90.1 us -> 348 us
  waiting for transfers between devices: 187 us -> 234 us
    psum x1 -> x2, blocking collectives: 90.1 us -> 348 us  [the longest x1 346 us: body(): lax.psum((sum_gain, sum_qkv, sum_out), 'seq')]
    psum x1 -> x2, waiting for transfers between devices: 175 us -> 227 us  [the longest x1 227 us: body(): lax.psum((sum_gain, sum_qkv, sum_out), 'seq')]
  transfers between devices with their start and end apart: 17 -> 18, of which waited for: 5 -> 4; matrix products, arithmetic and copies ran while one was open for 5% -> 18% of each run, Pallas kernels for 0% -> 0%
where the time goes in v1:
time: 813 us; the launch traced here: 802 us
  blocking collectives  348 us (43%)
  waiting for transfers between devices  234 us (29%)
  matrix products  105 us (13%)
  starting transfers between devices  54 us (7%)
  local copies, waits for them, and re-layouts  29.8 us (4%)
  other arithmetic  16.2 us (2%)
  between operations  15.3 us (2%)
    psum x1, blocking collectives, body(): lax.psum((sum_gain, sum_qkv, sum_out), 'seq')  346 us
    psum x1, waiting for transfers between devices, body(): lax.psum((sum_gain, sum_qkv, sum_out), 'seq')  227 us
    dot_general x20, matrix products, multiply(): return jnp.einsum(form, left, right, preferred_element_type=jnp.float32)  84.5 us
    ppermute x16, starting transfers between devices, from_behind(): return lax.ppermute(array, axis, pairs)  53.9 us
  transfers between devices with their start and end apart: 18, of which 4 were waited for; matrix products, arithmetic and copies ran while one was open for 18% of the time, Pallas kernels for 0%

profile of v1, /device:TPU:2, one launch (start us, length us, event | category | flops | bytes accessed | tf_op | source)
XLA Modules:
  0.0 802.0 jit_solution(11857781367051145466)
XLA Ops:
  11.0 6.2 collective-permute-start.2
  19.2 4.7 collective-permute-start.3
  33.1 4.3 scatter_custom_fusion
  38.3 4.2 collective-permute-start.10
  42.5 4.6 collective-permute-start.11
  51.7 6.1 collective-permute-start.7
  60.9 5.3 collective-permute-done.4
  66.2 5.7 collective-permute-start.6
  76.9 4.5 concatenate.46
  82.8 4.0 gather_fusion
  89.0 5.3 fusion.155
  94.4 4.4 fusion.50
  102.2 4.5 fusion.157
  106.7 14.7 %fusion.44 = bf16[8,32,512]{2,1,0:T(8,128)(2,1)} fusion(bf16[512,8,32]{0,2,1:T(8,128)(2,1)S(1)} %bitcast.270, f32[8,512,512]{1,2,0:T(8,128)} %fusion.157, f32[8,512,512]{1,2,0:T(8,128)} %get-tuple-element.81, f32[8,512]{1,0:T(8,128)S(1)} %get-tuple-element.80), kind=kOutput, calls=%fused_computation.48 | convolution fusion | flops 149033472 | bytes 17317888 | tf_op jit(solution)/shard_map/hqk,khd->qhd/dot_general | solution.py:21
  121.4 12.8 %fusion.47 = bf16[8,32,512]{2,1,0:T(8,128)(2,1)} fusion(bf16[512,8,32]{0,2,1:T(8,128)(2,1)S(1)} %bitcast.272, f32[8,512,512]{1,2,0:T(8,128)} %fusion.157, f32[8,512,512]{1,2,0:T(8,128)} %get-tuple-element.81, f32[8,512]{1,0:T(8,128)S(1)} %get-tuple-element.80), kind=kOutput, calls=%fused_computation.49 | convolution fusion | flops 149033472 | bytes 17317888 | tf_op jit(solution)/shard_map/hqk,qhd->khd/dot_general | solution.py:21
  135.3 5.3 fusion.156
  140.6 5.6 fusion.59
  147.2 4.5 fusion.158
  151.7 14.7 %fusion.38 = bf16[8,32,512]{2,1,0:T(8,128)(2,1)} fusion(bf16[512,8,32]{0,2,1:T(8,128)(2,1)S(1)} %bitcast.274, f32[8,512,512]{1,2,0:T(8,128)} %fusion.158, f32[8,512,512]{1,2,0:T(8,128)} %get-tuple-element.83, f32[8,512]{1,0:T(8,128)S(1)} %get-tuple-element.82), kind=kOutput, calls=%fused_computation.46 | convolution fusion | flops 149033472 | bytes 17317888 | tf_op jit(solution)/shard_map/hqk,khd->qhd/dot_general | solution.py:21
  166.4 12.9 %fusion.41 = bf16[8,32,512]{2,1,0:T(8,128)(2,1)} fusion(bf16[512,8,32]{0,2,1:T(8,128)(2,1)S(1)} %bitcast.276, f32[8,512,512]{1,2,0:T(8,128)} %fusion.158, f32[8,512,512]{1,2,0:T(8,128)} %get-tuple-element.83, f32[8,512]{1,0:T(8,128)S(1)} %get-tuple-element.82), kind=kOutput, calls=%fused_computation.47 | convolution fusion | flops 149033472 | bytes 17317888 | tf_op jit(solution)/shard_map/hqk,qhd->khd/dot_general | solution.py:21
  194.5 226.8 %all-reduce.5.cloned.1.call-done = (f32[256,768]{1,0:T(8,128)}, f32[256,256]{1,0:T(8,128)}) async-done(((f32[256,768]{1,0:T(8,128)}, f32[256,256]{1,0:T(8,128)}), (f32[256,768]{1,0:T(8,128)}, f32[256,256]{1,0:T(8,128)})) %all-reduce.5.cloned.1.call-update) | async-done | bytes 1048592 | tf_op jit(solution)/shard_map/psum | solution.py:201
  422.8 4.0 collective-permute-start.15
  435.3 345.9 %psum.42 = f32[256]{0:T(256)S(1)} all-reduce(f32[256]{0:T(256)S(1)} %add.185), channel_id=1, replica_groups=mesh['seq'=128,'batch'=2] {'seq'}, use_global_device_ids=true, to_apply=%region_43.44 | all-reduce | flops 256 | bytes 2048 | tf_op jit(solution)/shard_map/psum | solution.py:201
  784.9 4.5 concatenate.52
  (215 shorter events, 71.4 us)
Async XLA Ops:
  7.2 80.8 %copy-start = (bf16[256,768]{1,0:T(8,128)(2,1)S(1)}, bf16[256,768]{1,0:T(8,128)(2,1)}, u32[]{:S(2)}) copy-start(bf16[256,768]{1,0:T(8,128)(2,1)} %param.10) | copy-start | bytes 1179652
  7.2 414.1 %all-reduce.5.cloned.1.call-start = ((), (), s32[]{:S(2)}) async-start(), calls=%async_computation | async-start | bytes 2097152 | tf_op jit(solution)/shard_map/psum | solution.py:201
  9.6 28.7 %collective-permute-start = (bf16[2,2]{1,0:T(2,128)(2,1)S(1)}, bf16[2,2]{1,0:T(2,128)(2,1)S(1)}, u32[]{:S(2)}, u32[]{:S(2)}) collective-permute-start(bf16[2,2]{1,0:T(2,128)(2,1)S(1)} %pad_maximum_fusion.6), channel_id=1, source_target_pairs={{4,0},{6,2},{8,4},{10,6},{12,8},{14,10},{16,12},{18,14},{20,16},{2... | collective-permute-start | bytes 32 | tf_op jit(solution)/shard_map/ppermute | solution.py:17
  11.0 31.6 %collective-permute-start.2 = (bf16[2,2]{1,0:T(2,128)(2,1)S(1)}, bf16[2,2]{1,0:T(2,128)(2,1)S(1)}, u32[]{:S(2)}, u32[]{:S(2)}) collective-permute-start(bf16[2,2]{1,0:T(2,128)(2,1)S(1)} %pad_maximum_fusion.8), channel_id=1, source_target_pairs={{0,2},{2,4},{4,6},{6,8},{8,10},{10,12},{12,14},{14,16},{16,18},{18... | collective-permute-start | bytes 32 | tf_op jit(solution)/shard_map/ppermute | solution.py:17
  17.2 29.9 %collective-permute-start.1 = (bf16[2,2]{1,0:T(2,128)(2,1)S(1)}, bf16[2,2]{1,0:T(2,128)(2,1)S(1)}, u32[]{:S(2)}, u32[]{:S(2)}) collective-permute-start(bf16[2,2]{1,0:T(2,128)(2,1)S(1)} %pad_maximum_fusion.7), channel_id=1, source_target_pairs={{2,0},{4,2},{6,4},{8,6},{10,8},{12,10},{14,12},{16,14},{18,16},{20... | collective-permute-start | bytes 32 | tf_op jit(solution)/shard_map/ppermute | solution.py:17
  19.2 29.3 %collective-permute-start.3 = (bf16[2,2]{1,0:T(2,128)(2,1)S(1)}, bf16[2,2]{1,0:T(2,128)(2,1)S(1)}, u32[]{:S(2)}, u32[]{:S(2)}) collective-permute-start(bf16[2,2]{1,0:T(2,128)(2,1)S(1)} %pad_maximum_fusion.9), channel_id=1, source_target_pairs={{0,4},{2,6},{4,8},{6,10},{8,12},{10,14},{12,16},{14,18},{16,20},{1... | collective-permute-start | bytes 32 | tf_op jit(solution)/shard_map/ppermute | solution.py:17
  27.0 49.1 %collective-permute-start.9 = (bf16[2,128,512]{2,0,1:T(2,128)(2,1)S(1)}, bf16[2,128,512]{2,0,1:T(2,128)(2,1)}, u32[]{:S(2)}, u32[]{:S(2)}) collective-permute-start(bf16[2,128,512]{2,0,1:T(2,128)(2,1)S(1)} %convolution_convert_fusion.12), channel_id=1, source_target_pairs={{2,0},{4,2},{6,4},{8,6},{10,8},{12,10},{14,12},{16,14},{18,16},{20... | collective-permute-start | bytes 786440 | tf_op jit(solution)/shard_map/ppermute | solution.py:17
  38.3 37.8 %collective-permute-start.10 = (bf16[2,128,512]{2,0,1:T(2,128)(2,1)S(1)}, bf16[2,128,512]{2,0,1:T(2,128)(2,1)}, u32[]{:S(2)}, u32[]{:S(2)}) collective-permute-start(bf16[2,128,512]{2,0,1:T(2,128)(2,1)S(1)} %convolution_convert_fusion.11), channel_id=1, source_target_pairs={{0,2},{2,4},{4,6},{6,8},{8,10},{10,12},{12,14},{14,16},{16,18},{18... | collective-permute-start | bytes 786440 | tf_op jit(solution)/shard_map/ppermute | solution.py:17
  42.5 33.6 %collective-permute-start.11 = (bf16[2,128,512]{2,0,1:T(2,128)(2,1)S(1)}, bf16[2,128,512]{2,0,1:T(2,128)(2,1)S(1)}, u32[]{:S(2)}, u32[]{:S(2)}) collective-permute-start(bf16[2,128,512]{2,0,1:T(2,128)(2,1)S(1)} %convolution_convert_fusion.10), channel_id=1, source_target_pairs={{0,4},{2,6},{4,8},{6,10},{8,12},{10,14},{12,16},{14,18},{16,20},{1... | collective-permute-start | bytes 786440 | tf_op jit(solution)/shard_map/ppermute | solution.py:17
  47.1 29.7 %collective-permute-start.8 = (bf16[2,128,512]{2,0,1:T(2,128)(2,1)S(1)}, bf16[2,128,512]{2,0,1:T(2,128)(2,1)}, u32[]{:S(2)}, u32[]{:S(2)}) collective-permute-start(bf16[2,128,512]{2,0,1:T(2,128)(2,1)S(1)} %convolution_convert_fusion.13), channel_id=1, source_target_pairs={{4,0},{6,2},{8,4},{10,6},{12,8},{14,10},{16,12},{18,14},{20,16},{2... | collective-permute-start | bytes 786440 | tf_op jit(solution)/shard_map/ppermute | solution.py:17
  51.7 7.3 collective-permute-start.7
  59.0 7.2 collective-permute-start.4
  66.2 7.0 collective-permute-start.6
  73.2 360.7 %collective-permute-start.5 = (bf16[2,2]{1,0:T(2,128)(2,1)}, bf16[2,2]{1,0:T(2,128)(2,1)}, u32[]{:S(2)}, u32[]{:S(2)}) collective-permute-start(bf16[2,2]{1,0:T(2,128)(2,1)} %pad_maximum_fusion.11), channel_id=1, source_target_pairs={{2,0},{4,2},{6,4},{8,6},{10,8},{12,10},{14,12},{16,14},{18,16},{20... | collective-permute-start | bytes 32 | tf_op jit(solution)/shard_map/ppermute | solution.py:17
  186.3 605.0 %all-reduce.7.cloned.1.call-start = ((), (), s32[]{:S(2)}) async-start(), calls=%async_computation.1 | async-start | bytes 2097152 | tf_op jit(solution)/shard_map/psum | solution.py:201
  187.4 233.9 %copy-start.11 = (pred[2,8]{1,0:T(4,128)(4,1)S(1)}, pred[2,8]{1,0:T(4,128)(4,1)}, u32[]{:S(2)}) copy-start(pred[2,8]{1,0:T(4,128)(4,1)} %get-tuple-element.43) | copy-start | bytes 52
  187.5 247.0 %copy-start.14 = (s32[8]{0:T(128)S(1)}, s32[8]{0:T(128)}, u32[]{:S(2)}) copy-start(s32[8]{0:T(128)} %get-tuple-element.63) | copy-start | bytes 100
  187.5 247.0 %copy-start.16 = (s32[2]{0:T(128)S(1)}, s32[2]{0:T(128)}, u32[]{:S(2)}) copy-start(s32[2]{0:T(128)} %add_bitcast_fusion) | copy-start | bytes 28
  187.5 247.0 %copy-start.17 = (s32[2]{0:T(128)S(1)}, s32[2]{0:T(128)}, u32[]{:S(2)}) copy-start(s32[2]{0:T(128)} %add_bitcast_fusion.6) | copy-start | bytes 28
  187.5 247.0 %copy-start.18 = (s32[2]{0:T(128)S(1)}, s32[2]{0:T(128)}, u32[]{:S(2)}) copy-start(s32[2]{0:T(128)} %add_bitcast_fusion.2) | copy-start | bytes 28
  422.8 361.4 %collective-permute-start.15 = (bf16[2,128,512]{2,0,1:T(2,128)(2,1)}, bf16[2,128,512]{2,0,1:T(2,128)(2,1)S(1)}, u32[]{:S(2)}, u32[]{:S(2)}) collective-permute-start(bf16[2,128,512]{2,0,1:T(2,128)(2,1)} %convolution_convert_fusion.4), channel_id=1, source_target_pairs={{0,4},{2,6},{4,8},{6,10},{8,12},{10,14},{12,16},{14,18},{16,20},{1... | collective-permute-start | bytes 786440 | tf_op jit(solution)/shard_map/ppermute | solution.py:17
  426.8 357.4 %collective-permute-start.14 = (bf16[2,128,512]{2,0,1:T(2,128)(2,1)S(1)}, bf16[2,128,512]{2,0,1:T(2,128)(2,1)S(1)}, u32[]{:S(2)}, u32[]{:S(2)}) collective-permute-start(bf16[2,128,512]{2,0,1:T(2,128)(2,1)S(1)} %convolution_convert_fusion.5), channel_id=1, source_target_pairs={{0,2},{2,4},{4,6},{6,8},{8,10},{10,12},{12,14},{14,16},{16,18},{18... | collective-permute-start | bytes 786440 | tf_op jit(solution)/shard_map/ppermute | solution.py:17
  428.7 355.4 %collective-permute-start.13 = (bf16[2,128,512]{2,0,1:T(2,128)(2,1)S(1)}, bf16[2,128,512]{2,0,1:T(2,128)(2,1)}, u32[]{:S(2)}, u32[]{:S(2)}) collective-permute-start(bf16[2,128,512]{2,0,1:T(2,128)(2,1)S(1)} %convolution_convert_fusion.6), channel_id=1, source_target_pairs={{2,0},{4,2},{6,4},{8,6},{10,8},{12,10},{14,12},{16,14},{18,16},{20... | collective-permute-start | bytes 786440 | tf_op jit(solution)/shard_map/ppermute | solution.py:17
  432.6 352.3 %collective-permute-start.12 = (bf16[2,128,512]{2,0,1:T(2,128)(2,1)}, bf16[2,128,512]{2,0,1:T(2,128)(2,1)}, u32[]{:S(2)}, u32[]{:S(2)}) collective-permute-start(bf16[2,128,512]{2,0,1:T(2,128)(2,1)} %convolution_convert_fusion.7), channel_id=1, source_target_pairs={{4,0},{6,2},{8,4},{10,6},{12,8},{14,10},{16,12},{18,14},{20,16},{2... | collective-permute-start | bytes 786440 | tf_op jit(solution)/shard_map/ppermute | solution.py:17
  (21 other events, 163.4 us)
Sparse Core Ops, SparseCore 0:
  186.4 234.8 all-reduce.4
  423.9 27.6 all-reduce.6
